TPU v7x, 128 devices: a whole 4x4x4 slice. The times are simulated.
128 devices in a mesh: row: 16 (over y_lo, x, core), col: 8 (over y_hi, z).
Axes of the slice: x: 4, y: 4 (y_hi: 2, y_lo: 2; y = y_hi * 2 + y_lo), z: 4, core: 2. Of those that a mesh axis runs over, the one named last changes fastest.
Arguments:
- density: bfloat16 [6144, 6144], P(('row', 'col')), may hold values from -0.49023438 to 0.49023438
- pattern: int32 [48, 48], replicated, may hold values 0 or 1
- filter_square: int32 [48, 48], replicated, may hold values 0 or 1
- filter_cube: int32 [48, 48], replicated, may hold values 0 or 1
Outputs:
- purified: float32 [6144, 6144], P('row', 'col')
All inputs are finite; a program needn't handle non-finite values.
Results may differ from a plain program's by a relative error of at most 0.0027.
Values may be sent and summed in bfloat16 or wider, within the bound.
A program may use at most 64 MiB of HBM per device.

v0:
```python
import jax
import jax.numpy as jnp
from jax import lax
from jax.sharding import PartitionSpec as P

BLK = 128


def tile_mask(mask, row_id, col_id, rows, width):
    row_blocks = rows // BLK
    col_blocks = width // BLK
    small = lax.dynamic_slice(
        mask, (row_id * row_blocks, col_id * col_blocks), (row_blocks, col_blocks)
    ).astype(jnp.float32)
    return jnp.broadcast_to(small[:, None, :, None], (row_blocks, BLK, col_blocks, BLK)).reshape(
        rows, width
    )


def on_device(density, pattern, filter_square, filter_cube):
    row_count = lax.axis_size("row")
    col_count = lax.axis_size("col")
    row_id = lax.axis_index("row")
    col_id = lax.axis_index("col")
    rows_one, order = density.shape
    nblocks = pattern.shape[0]
    rows = order // row_count
    width = order // col_count
    first = (row_id * col_count + col_id) * rows_one
    block_of = (first + jnp.arange(rows_one, dtype=jnp.int32)) // BLK
    row_mask = jnp.take(pattern, block_of, axis=0).astype(jnp.bfloat16)
    full_mask = jnp.broadcast_to(row_mask[:, :, None], (rows_one, nblocks, BLK)).reshape(
        rows_one, order
    )
    local = density * full_mask
    left = lax.all_gather(local, "col", axis=0, tiled=True)
    tile = lax.dynamic_slice(left, (0, col_id * width), (rows, width))
    right = lax.all_gather(tile, "row", axis=0, tiled=True)
    square = jnp.dot(left, right, preferred_element_type=jnp.float32)
    square = square * tile_mask(filter_square, row_id, col_id, rows, width)
    half = lax.all_gather(square.astype(jnp.bfloat16), "row", axis=0, tiled=True)
    cube = jnp.dot(left, half, preferred_element_type=jnp.float32)
    cube = cube * tile_mask(filter_cube, row_id, col_id, rows, width)
    return 3.0 * square - 2.0 * cube


def solution(mesh):
    placed = (P(("row", "col"), None), P(), P(), P())
    return jax.shard_map(
        on_device, mesh=mesh, in_specs=placed, out_specs=P("row", "col"), check_vma=False
    )
```

profile of v0, /device:TPU:1, one launch (start us, length us, event | category | flops | bytes accessed | tf_op | source)
XLA Modules:
  0.0 231.8 jit_solution(9919951318664396545)
XLA Ops:
  6.5 0.0 copy-start
  6.5 0.0 all-gather.4.cloned.1.call-start
  6.6 0.7 copy-done
  7.3 0.6 gather_fusion
  7.9 0.1 select_convert_fusion
  7.9 0.4 broadcast_in_dim.30
  8.3 2.0 bitcast_multiply_fusion
  10.3 0.0 all-gather.4.cloned.1.call-update
  10.4 0.0 all-gather.6.cloned.1.call-start
  10.4 78.9 %all-gather.4.cloned.1.call-done = bf16[384,6144]{1,0:T(8,128)(2,1)} async-done(((bf16[48,6144]{1,0:T(8,128)(2,1)}), bf16[384,6144]{1,0:T(8,128)(2,1)}) %all-gather.4.cloned.1.call-update) | async-done | bytes 4718608 | tf_op jit(solution)/shard_map/all_gather | solution.py:36
  89.3 1.9 constant_dynamic-slice_fusion
  91.2 0.0 all-gather.6.cloned.1.call-update
  91.2 0.0 all-gather.8.cloned.1.call-start
  91.3 0.8 dynamic-slice_convert_fusion
  92.1 54.9 %all-gather.6.cloned.1.call-done = bf16[6144,768]{1,0:T(8,128)(2,1)} async-done(((bf16[384,768]{1,0:T(8,128)(2,1)}), bf16[6144,768]{1,0:T(8,128)(2,1)}) %all-gather.6.cloned.1.call-update) | async-done | bytes 9437200 | tf_op jit(solution)/shard_map/all_gather | solution.py:38
  146.9 0.2 broadcast_in_dim.31
  147.1 9.8 %fusion.3 = (bf16[384,768]{1,0:T(8,128)(2,1)}, f32[384,768]{1,0:T(8,128)S(1)}) fusion(f32[48,8,6,128]{3,2,1,0:T(8,128)S(1)} %bitcast.18, bf16[384,6144]{1,0:T(8,128)(2,1)} %all-gather.4.cloned.1.call-done, bf16[6144,768]{1,0:T(8,128)(2,1)} %all-gather.6.cloned.1.call-done), kind=kOutput, calls=%fused_computation.23 | convolution fusion | flops 3624468480 | bytes 17104896 | tf_op jit(solution)/shard_map/dot_general | solution.py:39
  156.9 0.0 all-gather.8.cloned.1.call-update
  156.9 58.1 %all-gather.8.cloned.1.call-done = bf16[6144,768]{1,0:T(8,128)(2,1)} async-done(((bf16[384,768]{1,0:T(8,128)(2,1)}), bf16[6144,768]{1,0:T(8,128)(2,1)}) %all-gather.8.cloned.1.call-update) | async-done | bytes 9437200 | tf_op jit(solution)/shard_map/all_gather | solution.py:41
  215.0 0.2 broadcast_in_dim.32
  215.1 10.1 %fusion.1 = f32[384,768]{1,0:T(8,128)} fusion(bf16[384,6144]{1,0:T(8,128)(2,1)} %all-gather.4.cloned.1.call-done, bf16[6144,768]{1,0:T(8,128)(2,1)} %all-gather.8.cloned.1.call-done, f32[48,8,6,128]{3,2,1,0:T(8,128)S(1)} %bitcast.19, f32[384,768]{1,0:T(8,128)S(1)} %get-tuple-element.6), kind=kOutput, calls=%fused_computation.4 | convolution fusion | flops 3625058304 | bytes 17694720 | tf_op jit(solution)/shard_map/dot_general | solution.py:42
  (3 shorter events, 0.0 us)
Async XLA Ops:
  6.5 0.7 copy-start
  6.5 82.7 %all-gather.4.cloned.1.call-start = ((), (), s32[]{:S(2)}) async-start(), calls=%async_computation | async-start | bytes 5308416 | tf_op jit(solution)/shard_map/all_gather | solution.py:36
  10.4 136.6 %all-gather.6.cloned.1.call-start = ((), (), s32[]{:S(2)}) async-start(), calls=%async_computation.1 | async-start | bytes 10027008 | tf_op jit(solution)/shard_map/all_gather | solution.py:38
  91.2 123.7 %all-gather.8.cloned.1.call-start = ((), (), s32[]{:S(2)}) async-start(), calls=%async_computation.2 | async-start | bytes 10027008 | tf_op jit(solution)/shard_map/all_gather | solution.py:41
Sparse Core Ops, SparseCore 0:
  10.5 78.7 all-gather.3
  91.3 55.5 all-gather.5
  157.0 57.8 all-gather.7
where the time goes:
time: 232 us
  waiting for transfers between devices  192 us (83%)
  matrix products  19.9 us (9%)
  between operations  13.2 us (6%)
  local copies, waits for them, and re-layouts  3.89 us (2%)
  other arithmetic  2.93 us (1%)
    all_gather x1, waiting for transfers between devices, on_device(): left = lax.all_gather(local, 'col', axis=0, tiled=True)  78.9 us
    all_gather x1, waiting for transfers between devices, on_device(): lax.all_gather(square.astype(jnp.bfloat16), 'row', axis=0, tiled=True)  58.1 us
    all_gather x1, waiting for transfers between devices, on_device(): right = lax.all_gather(tile, 'row', axis=0, tiled=True)  54.9 us
    dot_general x1, matrix products, on_device(): cube = jnp.dot(left, half, preferred_element_type=jnp.float32)  10.1 us
    dot_general x1, matrix products, on_device(): square = jnp.dot(left, right, preferred_element_type=jnp.float32)  9.77 us
  transfers between devices with their start and end apart: 3, of which 3 were waited for; matrix products, arithmetic and copies ran while one was open for 0% of the time, Pallas kernels for 0%

commit v1 on v0

--- a/solution.py
+++ b/solution.py
@@ -33,7 +33,9 @@
         rows_one, order
     )
     local = density * full_mask
-    left = lax.all_gather(local, "col", axis=0, tiled=True)
+    left = jnp.concatenate(
+        lax.all_to_all(jnp.stack([local] * lax.axis_size("col")), "col", 0, 0), axis=0
+    )
     tile = lax.dynamic_slice(left, (0, col_id * width), (rows, width))
     right = lax.all_gather(tile, "row", axis=0, tiled=True)
     square = jnp.dot(left, right, preferred_element_type=jnp.float32)

time: 232 us -> 220 us (0.948)
  waiting for transfers between devices: 192 us -> 169 us
  starting transfers between devices: 0.09 us -> 8.57 us
  local copies, waits for them, and re-layouts: 3.89 us -> 6.6 us
    all_gather x1 -> x0, waiting for transfers between devices: 78.9 us -> none  [on_device(): left = lax.all_gather(local, 'col', axis=0, tiled=True)]
    all_to_all x0 -> x1, waiting for transfers between devices: none -> 54.3 us  [on_device(): lax.all_to_all(jnp.stack([local] * lax.axis_size('col')), 'col', 0, 0)]
    all_to_all x0 -> x1, starting transfers between devices: none -> 8.49 us  [on_device(): lax.all_to_all(jnp.stack([local] * lax.axis_size('col')), 'col', 0, 0)]
    another operation x0 -> x1, local copies, waits for them, and re-layouts: none -> 2.7 us  [on_device(): jnp.stack([local] * lax.axis_size('col'))]
where the time goes in v1:
time: 220 us; the launch traced here: 219 us
  waiting for transfers between devices  169 us (77%)
  matrix products  19.9 us (9%)
  between operations  13.5 us (6%)
  starting transfers between devices  8.57 us (4%)
  local copies, waits for them, and re-layouts  6.6 us (3%)
    all_gather x1, waiting for transfers between devices, on_device(): lax.all_gather(square.astype(jnp.bfloat16), 'row', axis=0, tiled=True)  58.1 us
    all_gather x1, waiting for transfers between devices, on_device(): right = lax.all_gather(tile, 'row', axis=0, tiled=True)  56.5 us
    all_to_all x1, waiting for transfers between devices, on_device(): lax.all_to_all(jnp.stack([local] * lax.axis_size('col')), 'col', 0, 0)  54.3 us
    dot_general x1, matrix products, on_device(): cube = jnp.dot(left, half, preferred_element_type=jnp.float32)  10.1 us
    dot_general x1, matrix products, on_device(): square = jnp.dot(left, right, preferred_element_type=jnp.float32)  9.77 us
    all_to_all x1, starting transfers between devices, on_device(): lax.all_to_all(jnp.stack([local] * lax.axis_size('col')), 'col', 0, 0)  8.49 us
  transfers between devices with their start and end apart: 3, of which 3 were waited for; matrix products, arithmetic and copies ran while one was open for 0% of the time, Pallas kernels for 0%

profile of v1, /device:TPU:1, one launch (start us, length us, event | category | flops | bytes accessed | tf_op | source)
XLA Modules:
  0.0 219.5 jit_solution(2784126029004024277)
XLA Ops:
  6.5 0.0 copy-start
  6.6 0.7 copy-done
  7.3 0.6 gather_fusion
  7.9 0.1 select_convert_fusion
  7.9 0.4 broadcast_in_dim.30
  8.3 1.2 bitcast_multiply_fusion
  9.5 2.7 %stack.2 = bf16[8,48,6144]{2,1,0:T(8,128)(2,1)} broadcast(bf16[48,6144]{1,0:T(8,128)(2,1)S(1)} %bitcast_multiply_fusion), dimensions={1,2} | broadcast | bytes 5308416 | tf_op jit(solution)/shard_map/stack | solution.py:37
  12.2 8.5 %all-to-all-start = ((bf16[8,48,6144]{2,1,0:T(8,128)(2,1)}), bf16[8,48,6144]{2,1,0:T(8,128)(2,1)}, u32[]{:S(2)}, u32[]{:S(2)}) async-start(bf16[8,48,6144]{2,1,0:T(8,128)(2,1)} %stack.2), calls=%async_computation | async-start | bytes 9437184 | tf_op jit(solution)/shard_map/all_to_all | solution.py:37
  20.7 0.0 all-gather.3.cloned.1.call-start
  20.8 54.3 %all-to-all-done = bf16[8,48,6144]{2,1,0:T(8,128)(2,1)} async-done(((bf16[8,48,6144]{2,1,0:T(8,128)(2,1)}), bf16[8,48,6144]{2,1,0:T(8,128)(2,1)}, u32[]{:S(2)}, u32[]{:S(2)}) %all-to-all-start) | async-done | bytes 4718624 | tf_op jit(solution)/shard_map/all_to_all | solution.py:37
  75.1 1.9 constant_dynamic-slice_fusion
  77.0 0.0 all-gather.3.cloned.1.call-update
  77.0 0.0 all-gather.5.cloned.1.call-start
  77.0 0.8 dynamic-slice_convert_fusion
  77.8 56.5 %all-gather.3.cloned.1.call-done = bf16[6144,768]{1,0:T(8,128)(2,1)} async-done(((bf16[384,768]{1,0:T(8,128)(2,1)}), bf16[6144,768]{1,0:T(8,128)(2,1)}) %all-gather.3.cloned.1.call-update) | async-done | bytes 9437200 | tf_op jit(solution)/shard_map/all_gather | solution.py:40
  134.3 0.2 broadcast_in_dim.31
  134.5 9.8 %fusion.3 = (bf16[384,768]{1,0:T(8,128)(2,1)}, f32[384,768]{1,0:T(8,128)S(1)}) fusion(f32[48,8,6,128]{3,2,1,0:T(8,128)S(1)} %bitcast.19, bf16[384,6144]{1,0:T(8,128)(2,1)} %bitcast.1, bf16[6144,768]{1,0:T(8,128)(2,1)} %all-gather.3.cloned.1.call-done), kind=kOutput, calls=%fused_computation.23 | convolution fusion | flops 3624468480 | bytes 17104896 | tf_op jit(solution)/shard_map/dot_general | solution.py:41
  144.3 0.0 all-gather.5.cloned.1.call-update
  144.3 58.1 %all-gather.5.cloned.1.call-done = bf16[6144,768]{1,0:T(8,128)(2,1)} async-done(((bf16[384,768]{1,0:T(8,128)(2,1)}), bf16[6144,768]{1,0:T(8,128)(2,1)}) %all-gather.5.cloned.1.call-update) | async-done | bytes 9437200 | tf_op jit(solution)/shard_map/all_gather | solution.py:43
  202.4 0.2 broadcast_in_dim.32
  202.5 10.1 %fusion.1 = f32[384,768]{1,0:T(8,128)} fusion(bf16[384,6144]{1,0:T(8,128)(2,1)} %bitcast.1, bf16[6144,768]{1,0:T(8,128)(2,1)} %all-gather.5.cloned.1.call-done, f32[48,8,6,128]{3,2,1,0:T(8,128)S(1)} %bitcast.20, f32[384,768]{1,0:T(8,128)S(1)} %get-tuple-element.6), kind=kOutput, calls=%fused_computation.4 | convolution fusion | flops 3625058304 | bytes 17694720 | tf_op jit(solution)/shard_map/dot_general | solution.py:44
  (3 shorter events, 0.0 us)
Async XLA Ops:
  6.5 0.7 copy-start
  12.2 62.8 %all-to-all-start = ((bf16[8,48,6144]{2,1,0:T(8,128)(2,1)}), bf16[8,48,6144]{2,1,0:T(8,128)(2,1)}, u32[]{:S(2)}, u32[]{:S(2)}) async-start(bf16[8,48,6144]{2,1,0:T(8,128)(2,1)} %stack.2), calls=%async_computation | async-start | bytes 9437184 | tf_op jit(solution)/shard_map/all_to_all | solution.py:37
  20.7 113.6 %all-gather.3.cloned.1.call-start = ((), (), s32[]{:S(2)}) async-start(), calls=%async_computation.1 | async-start | bytes 10027008 | tf_op jit(solution)/shard_map/all_gather | solution.py:40
  77.0 125.4 %all-gather.5.cloned.1.call-start = ((), (), s32[]{:S(2)}) async-start(), calls=%async_computation.2 | async-start | bytes 10027008 | tf_op jit(solution)/shard_map/all_gather | solution.py:43
Sparse Core Ops, SparseCore 0:
  77.1 57.1 all-gather.2
  144.4 57.8 all-gather.4
